TPU v7x, 32 devices: a whole 2x2x4 slice. The times are simulated.
32 devices in a mesh: band: 4 (over x, core), row: 8 (over z, y).
Axes of the slice: x: 2, y: 2, z: 4, core: 2. Of those that a mesh axis runs over, the one named last changes fastest.
Arguments:
- shape_coupling_matrices: bfloat16 [512, 4, 128, 128], P('row'), may hold values from 0 to 0.00390625
- target_strip_index: int32 [512, 4], P('row'), may hold values from 0 to 511, as said below
- occupied_entries_per_strip: int32 [512], P('row'), may hold values from 1 to 4
- prior_leaving_energy: bfloat16 [4, 65536], P('band', 'row'), may hold values from 0.19921875 to 3
- facet_kelvins: float32 [65536], P('row'), may hold values from 0.6 to 1.6
- emitting_ability: float32 [4, 65536], P('band', 'row'), may hold values from 0.2 to 0.9
- centre_frequency: float32 [4], P('band'), may hold values from 0.28 to 6.3
- frequency_span: float32 [4], P('band'), may hold values from 0.5 to 1.5
- prescribed_power_density: float32 [65536], P('row'), may hold values from -6 to 6
Outputs:
- corrected_kelvins: float32 [65536], P('row')
- refreshed_leaving_energy: float32 [4, 65536], P('band', 'row')
Inputs may be any that keep to these rules, and one draw needn't show every extreme that they name: `target_strip_index`: of the 256 entries of one device's rows, exactly 32 name a column tile held by each index of row.
All inputs are finite; a program needn't handle non-finite values.
Results may differ from a plain program's by a relative error of at most 0.0003.
Values may be sent and summed in bfloat16 or wider, within the bound.
No kernel may reach another device: no remote copies, remote signals or barrier semaphores. Data moves between devices by JAX's collectives and lax.ppermute only.
A program may use at most 64 MiB of HBM per device.

v0:
```python
import jax
import jax.numpy as jnp
from jax import lax
from jax.sharding import PartitionSpec as P


def emitter_terms(centre_sample, frequency_spacing, facet_kelvins):
    return (
        frequency_spacing[:, None]
        * centre_sample[:, None] ** 3
        / jnp.expm1(centre_sample[:, None] / facet_kelvins[None, :])
    )


def on_device(
    shape_coupling_matrices,
    target_strip_index,
    occupied_entries_per_strip,
    prior_leaving_energy,
    facet_kelvins,
    emitting_ability,
    centre_frequency,
    frequency_span,
    prescribed_power_density,
):
    bands_here, facets_here = prior_leaving_energy.shape
    tile_rows, slot_count = target_strip_index.shape
    tile_size = shape_coupling_matrices.shape[2]
    entries = tile_rows * slot_count
    flat_cols = target_strip_index.reshape(entries)
    gathered = lax.all_gather(prior_leaving_energy, "row", axis=1, tiled=True)
    picked = gathered.reshape(bands_here, -1, tile_size)[:, flat_cols]
    picked = picked.reshape(bands_here, tile_rows, slot_count, tile_size)
    slot_used = (
        lax.broadcasted_iota(jnp.int32, (tile_rows, slot_count), 1)
        < occupied_entries_per_strip[:, None]
    )
    masked = jnp.where(slot_used[None, :, :, None], picked, jnp.zeros_like(picked))
    incoming = jnp.einsum(
        "rkij,brkj->bri", shape_coupling_matrices, masked, preferred_element_type=jnp.float32
    ).reshape(bands_here, facets_here)
    partial_terms = emitter_terms(centre_frequency, frequency_span, facet_kelvins)
    planck_sum = lax.psum(jnp.sum(partial_terms, 0), "band")
    energy_portion = partial_terms / planck_sum
    kelvins_third_power = facet_kelvins**3
    ideal_emitter_power = energy_portion * kelvins_third_power * facet_kelvins
    refreshed_leaving_energy = (
        emitting_ability * ideal_emitter_power + (1.0 - emitting_ability) * incoming
    )
    quotient = emitting_ability / (1.0 - emitting_ability)
    flux_part = jnp.sum(quotient * (ideal_emitter_power - refreshed_leaving_energy), 0)
    gradient_piece = jnp.sum(quotient * 4.0 * energy_portion * kelvins_third_power, 0)
    balance_power_density, power_gradient = lax.psum((flux_part, gradient_piece), "band")
    corrected_kelvins = (
        facet_kelvins - (balance_power_density - prescribed_power_density) / power_gradient
    )
    return (corrected_kelvins, refreshed_leaving_energy)


def solution(mesh):
    in_specs = (
        P("row", None, None, None),
        P("row", None),
        P("row"),
        P("band", "row"),
        P("row"),
        P("band", "row"),
        P("band"),
        P("band"),
        P("row"),
    )
    out_specs = (P("row"), P("band", "row"))
    return jax.shard_map(
        on_device, mesh=mesh, in_specs=in_specs, out_specs=out_specs, check_vma=False
    )
```

profile of v0, /device:TPU:0, one launch (start us, length us, event | category | flops | bytes accessed | tf_op | source)
XLA Modules:
  0.0 104.3 jit_solution(12224050853336227778)
XLA Ops:
  7.2 0.0 copy-start
  7.2 0.0 copy-start.1
  7.2 0.0 all-reduce.3.cloned.1.call-start
  8.5 0.8 broadcast_divide_fusion
  9.3 12.9 %psum.21 = f32[8192]{0:T(1024)S(1)} all-reduce(f32[8192]{0:T(1024)S(1)} %broadcast_divide_fusion), channel_id=1, replica_groups=mesh['band'=4,'row'=8] {'band'}, use_global_device_ids=true, to_apply=%region_0.1 | all-reduce | flops 8192 | bytes 65536 | tf_op jit(solution)/shard_map/psum | solution.py:43
  22.2 31.3 %all_gather.3 = bf16[1,65536]{1,0:T(2,128)(2,1)S(1)} all-gather(bf16[1,8192]{1,0:T(2,128)(2,1)} %param.12), channel_id=1, replica_groups=mesh['band'=4,'row'=8] {'row'}, dimensions={1}, use_global_device_ids=true | all-gather | bytes 147456 | tf_op jit(solution)/shard_map/all_gather | solution.py:31
  53.5 0.8 copy.11
  54.3 0.1 reshape.85
  54.4 0.7 iota_compare_fusion
  55.1 0.8 multiply_multiply_fusion.2
  55.9 0.8 reduce
  56.7 0.9 gather_fusion
  57.6 0.1 select_bitcast_fusion
  57.7 6.3 %subtract_multiply_fusion = (f32[1,8192]{1,0:T(1,128)}, f32[1,8192]{1,0:T(1,128)S(1)}, f32[1,8192]{1,0:T(1,128)}) fusion(f32[1,8192]{1,0:T(1,128)S(1)} %bitcast.36, f32[1,8192]{1,0:T(1,128)} %param.14, bf16[64,4,128,128]{3,2,1,0:T(8,128)(2,1)} %param.9, bf16[64,4,128,1]{2,1,0,3:T(4,128)(2,1)S(1)} %select_bitcast_fusion), kind=kOutput, calls=%fused_computation.10 | convolution fusion | flops 8445952 | bytes 8617984 | tf_op jit(solution)/shard_map/rkij,brkj->bri/dot_general | solution.py:39
  64.0 0.7 multiply_multiply_fusion.1
  64.7 0.0 all-reduce.3.cloned.1.call-update
  64.7 31.3 %all-reduce.3.cloned.1.call-done = (f32[8192]{0:T(1024)}, f32[8192]{0:T(1024)}) async-done(((f32[8192]{0:T(1024)}, f32[8192]{0:T(1024)}), (f32[8192]{0:T(1024)}, f32[8192]{0:T(1024)})) %all-reduce.3.cloned.1.call-update) | async-done | bytes 65552 | tf_op jit(solution)/shard_map/psum | solution.py:53
  96.0 0.0 copy-done
  96.0 0.0 copy-done.1
  96.0 1.4 %divide_subtract_fusion = f32[8192]{0:T(1024)} fusion(f32[8192]{0:T(1024)S(1)} %copy-done, f32[8192]{0:T(1024)} %get-tuple-element.2, f32[8192]{0:T(1024)} %get-tuple-element.3, f32[8192]{0:T(1024)S(1)} %copy-done.1), kind=kLoop, calls=%fused_computation.8 | loop fusion | flops 24576 | bytes 163840 | tf_op jit(solution)/shard_map/sub | solution.py:55
  (2 shorter events, 0.0 us)
Async XLA Ops:
  7.2 88.8 %copy-start = (f32[8192]{0:T(1024)S(1)}, f32[8192]{0:T(1024)}, u32[]{:S(2)}) copy-start(f32[8192]{0:T(1024)} %param.13) | copy-start | bytes 98308
  7.2 88.8 %copy-start.1 = (f32[8192]{0:T(1024)S(1)}, f32[8192]{0:T(1024)}, u32[]{:S(2)}) copy-start(f32[8192]{0:T(1024)} %param.17) | copy-start | bytes 98308
  7.2 88.8 %all-reduce.3.cloned.1.call-start = ((), (), s32[]{:S(2)}) async-start(), calls=%async_computation | async-start | bytes 131072 | tf_op jit(solution)/shard_map/psum | solution.py:53
Sparse Core Ops, SparseCore 0:
  64.8 31.1 all-reduce.2
where the time goes:
time: 105 us; the launch traced here: 104 us
  blocking collectives  44.2 us (42%)
  waiting for transfers between devices  31.3 us (30%)
  between operations  15.4 us (15%)
  matrix products  6.3 us (6%)
  other arithmetic  5.3 us (5%)
  local copies, waits for them, and re-layouts  1.74 us (2%)
    psum x1, waiting for transfers between devices, on_device(): lax.psum((flux_part, gradient_piece), 'band')  31.3 us
    all_gather x1, blocking collectives, on_device(): gathered = lax.all_gather(prior_leaving_energy, 'row', axis=1, tiled=True)  31.3 us
    psum x1, blocking collectives, on_device(): planck_sum = lax.psum(jnp.sum(partial_terms, 0), 'band')  12.9 us
    dot_general x1, matrix products, on_device(): jnp.einsum('rkij,brkj->bri', shape_coupling_matrices, masked, preferred_e...  6.3 us
  transfers between devices with their start and end apart: 1, of which 1 were waited for; matrix products, arithmetic and copies ran while one was open for 0% of the time, Pallas kernels for 0%

commit v1 on v0

--- a/solution.py
+++ b/solution.py
@@ -2,6 +2,28 @@
 import jax.numpy as jnp
 from jax import lax
 from jax.sharding import PartitionSpec as P
+
+
+def in_order(blocks, dim):
+    blocks = jnp.moveaxis(blocks, 0, dim)
+    lengths = blocks.shape
+    return blocks.reshape(*lengths[:dim], lengths[dim] * lengths[dim + 1], *lengths[dim + 2 :])
+
+
+def collected_by_bits(array, axis):
+    size = lax.axis_size(axis)
+    parts = array[None]
+    for level in range(size.bit_length() - 1):
+        bit = 1 << level
+        other = lax.ppermute(parts, axis, [(i, i ^ bit) for i in range(size)])
+        both = jnp.stack([parts, other])
+        upper = lax.axis_index(axis) >> level & 1
+        parts = jnp.where(upper == 0, both, both[::-1]).reshape(-1, *array.shape)
+    return parts
+
+
+def gather_by_bits(x, axis, dim):
+    return in_order(collected_by_bits(x, axis), dim)
 
 
 def emitter_terms(centre_sample, frequency_spacing, facet_kelvins):
@@ -28,7 +50,7 @@
     tile_size = shape_coupling_matrices.shape[2]
     entries = tile_rows * slot_count
     flat_cols = target_strip_index.reshape(entries)
-    gathered = lax.all_gather(prior_leaving_energy, "row", axis=1, tiled=True)
+    gathered = gather_by_bits(prior_leaving_energy, "row", 1)
     picked = gathered.reshape(bands_here, -1, tile_size)[:, flat_cols]
     picked = picked.reshape(bands_here, tile_rows, slot_count, tile_size)
     slot_used = (

time: 105 us -> 87.2 us (0.83)
  blocking collectives: 44.2 us -> 10.8 us
  starting transfers between devices: 0.04 us -> 7.37 us
  waiting for transfers between devices: 31.3 us -> 36.7 us
  local copies, waits for them, and re-layouts: 1.74 us -> 3.61 us
  other arithmetic: 5.3 us -> 6.52 us
    all_gather x1 -> x0, blocking collectives: 31.3 us -> none  [on_device(): gathered = lax.all_gather(prior_leaving_energy, 'row', axis=1, tiled=True)]
    ppermute x0 -> x3, starting transfers between devices: none -> 7.33 us  [collected_by_bits(): other = lax.ppermute(parts, axis, [(i, i ^ bit) for i in range(size)])]
    ppermute x0 -> x3, waiting for transfers between devices: none -> 4.88 us  [collected_by_bits(): other = lax.ppermute(parts, axis, [(i, i ^ bit) for i in range(size)])]
    psum x1, blocking collectives: 12.9 us -> 10.8 us  [on_device(): planck_sum = lax.psum(jnp.sum(partial_terms, 0), 'band')]
    another operation x0 -> x4, other arithmetic: none -> 1.88 us  [collected_by_bits(): both = jnp.stack([parts, other])]
    rev x0 -> x1, local copies, waits for them, and re-layouts: none -> 1.65 us  [collected_by_bits(): parts = jnp.where(upper == 0, both, both[::-1]).reshape(-1, *array.shape)]
  transfers between devices with their start and end apart: 1 -> 4, of which waited for: 1 -> 3; matrix products, arithmetic and copies ran while one was open for 0% -> 4% of each run, Pallas kernels for 0% -> 0%
where the time goes in v1:
time: 87.2 us; the launch traced here: 86.7 us
  waiting for transfers between devices  36.7 us (42%)
  between operations  15.4 us (18%)
  blocking collectives  10.8 us (12%)
  starting transfers between devices  7.37 us (8%)
  other arithmetic  6.52 us (7%)
  matrix products  6.3 us (7%)
  local copies, waits for them, and re-layouts  3.61 us (4%)
    psum x1, waiting for transfers between devices, on_device(): lax.psum((flux_part, gradient_piece), 'band')  31.8 us
    psum x1, blocking collectives, on_device(): planck_sum = lax.psum(jnp.sum(partial_terms, 0), 'band')  10.8 us
    ppermute x3, starting transfers between devices, collected_by_bits(): other = lax.ppermute(parts, axis, [(i, i ^ bit) for i in range(size)])  7.33 us
    dot_general x1, matrix products, on_device(): jnp.einsum('rkij,brkj->bri', shape_coupling_matrices, masked, preferred_e...  6.3 us
    ppermute x3, waiting for transfers between devices, collected_by_bits(): other = lax.ppermute(parts, axis, [(i, i ^ bit) for i in range(size)])  4.88 us
    another operation x4, other arithmetic, collected_by_bits(): both = jnp.stack([parts, other])  1.88 us
  transfers between devices with their start and end apart: 4, of which 3 were waited for; matrix products, arithmetic and copies ran while one was open for 4% of the time, Pallas kernels for 0%

profile of v1, /device:TPU:0, one launch (start us, length us, event | category | flops | bytes accessed | tf_op | source)
XLA Modules:
  0.0 86.7 jit_solution(5238730422590684484)
XLA Ops:
  7.2 3.0 %collective-permute-start = (bf16[1,1,8192]{2,1,0:T(2,128)(2,1)}, bf16[1,1,8192]{2,1,0:T(2,128)(2,1)S(1)}, u32[]{:S(2)}, u32[]{:S(2)}) collective-permute-start(bf16[1,1,8192]{2,1,0:T(2,128)(2,1)} %bitcast.48), channel_id=1, source_target_pairs={{0,1},{1,0},{2,3},{3,2},{4,5},{5,4},{6,7},{7,6},{8,9},{9,8},{10,11... | collective-permute-start | bytes 49160 | tf_op jit(solution)/shard_map/ppermute | solution.py:18
  11.6 0.8 broadcast_divide_fusion
  12.4 10.8 %psum.21 = f32[8192]{0:T(1024)S(1)} all-reduce(f32[8192]{0:T(1024)S(1)} %broadcast_divide_fusion), channel_id=1, replica_groups=mesh['band'=4,'row'=8] {'band'}, use_global_device_ids=true, to_apply=%region_0.1 | all-reduce | flops 8192 | bytes 65536 | tf_op jit(solution)/shard_map/psum | solution.py:65
  23.2 0.8 multiply_multiply_fusion.2
  24.0 0.7 iota_compare_fusion
  24.7 0.8 copy.13
  25.5 0.1 reshape.89
  25.6 0.8 pad_maximum_fusion.2
  26.4 1.7 %rev.9 = bf16[2,1,1,8192]{3,0,2,1:T(2,128)(2,1)S(1)} reverse(bf16[2,1,1,8192]{3,0,2,1:T(2,128)(2,1)S(1)} %pad_maximum_fusion.2), dimensions={0} | reverse | bytes 65536 | tf_op jit(solution)/shard_map/rev | solution.py:21
  28.1 0.9 fusion.4
  29.0 1.6 %collective-permute-start.1 = (bf16[2,1,8192]{2,0,1:T(2,128)(2,1)S(1)}, bf16[2,1,8192]{2,0,1:T(2,128)(2,1)S(1)}, u32[]{:S(2)}, u32[]{:S(2)}) collective-permute-start(bf16[2,1,8192]{2,0,1:T(2,128)(2,1)S(1)} %get-tuple-element.9), channel_id=1, source_target_pairs={{0,2},{1,3},{2,0},{3,1},{4,6},{5,7},{6,4},{7,5},{8,10},{9,11},{10,... | collective-permute-start | bytes 98312 | tf_op jit(solution)/shard_map/ppermute | solution.py:18
  30.6 2.3 %collective-permute-done.1 = bf16[2,1,8192]{2,0,1:T(2,128)(2,1)S(1)} collective-permute-done((bf16[2,1,8192]{2,0,1:T(2,128)(2,1)S(1)}, bf16[2,1,8192]{2,0,1:T(2,128)(2,1)S(1)}, u32[]{:S(2)}, u32[]{:S(2)}) %collective-permute-start.1) | collective-permute-done | bytes 32800 | tf_op jit(solution)/shard_map/ppermute | solution.py:18
  32.9 0.1 pad_maximum_fusion.1
  33.1 2.7 %collective-permute-start.2 = (bf16[4,1,8192]{2,0,1:T(4,128)(2,1)S(1)}, bf16[4,1,8192]{2,0,1:T(4,128)(2,1)S(1)}, u32[]{:S(2)}, u32[]{:S(2)}) collective-permute-start(bf16[4,1,8192]{2,0,1:T(4,128)(2,1)S(1)} %reshape.88), channel_id=1, source_target_pairs={{0,4},{1,5},{2,6},{3,7},{4,0},{5,1},{6,2},{7,3},{8,12},{9,13},{10,... | collective-permute-start | bytes 196616 | tf_op jit(solution)/shard_map/ppermute | solution.py:18
  35.8 2.5 %collective-permute-done.2 = bf16[4,1,8192]{2,0,1:T(4,128)(2,1)S(1)} collective-permute-done((bf16[4,1,8192]{2,0,1:T(4,128)(2,1)S(1)}, bf16[4,1,8192]{2,0,1:T(4,128)(2,1)S(1)}, u32[]{:S(2)}, u32[]{:S(2)}) %collective-permute-start.2) | collective-permute-done | bytes 65568 | tf_op jit(solution)/shard_map/ppermute | solution.py:18
  38.4 0.1 pad_maximum_fusion
  38.5 0.1 reverse_select_fusion
  38.5 0.2 reshape.91
  38.7 0.9 gather_fusion
  39.6 0.1 select_bitcast_fusion
  39.7 6.3 %subtract_multiply_fusion = (f32[1,8192]{1,0:T(1,128)}, f32[1,8192]{1,0:T(1,128)S(1)}, f32[1,8192]{1,0:T(1,128)}) fusion(f32[1,8192]{1,0:T(1,128)S(1)} %bitcast.57, f32[1,8192]{1,0:T(1,128)} %param.14, bf16[64,4,128,128]{3,2,1,0:T(8,128)(2,1)} %param.9, bf16[64,4,128,1]{2,1,0,3:T(4,128)(2,1)S(1)} %select_bitcast_fusion), kind=kOutput, calls=%fused_computation.16 | convolution fusion | flops 8445952 | bytes 8617984 | tf_op jit(solution)/shard_map/rkij,brkj->bri/dot_general | solution.py:61
  46.0 0.7 multiply_multiply_fusion.1
  46.7 31.8 %all-reduce.3.cloned.1.call-done = (f32[8192]{0:T(1024)}, f32[8192]{0:T(1024)}) async-done(((f32[8192]{0:T(1024)}, f32[8192]{0:T(1024)}), (f32[8192]{0:T(1024)}, f32[8192]{0:T(1024)})) %all-reduce.3.cloned.1.call-update) | async-done | bytes 65552 | tf_op jit(solution)/shard_map/psum | solution.py:75
  78.5 1.4 %divide_subtract_fusion = f32[8192]{0:T(1024)} fusion(f32[8192]{0:T(1024)S(1)} %copy-done, f32[8192]{0:T(1024)} %get-tuple-element.2, f32[8192]{0:T(1024)} %get-tuple-element.3, f32[8192]{0:T(1024)S(1)} %copy-done.1), kind=kLoop, calls=%fused_computation.14 | loop fusion | flops 24576 | bytes 163840 | tf_op jit(solution)/shard_map/sub | solution.py:77
  (12 shorter events, 0.2 us)
Async XLA Ops:
  7.2 71.3 %copy-start = (f32[8192]{0:T(1024)S(1)}, f32[8192]{0:T(1024)}, u32[]{:S(2)}) copy-start(f32[8192]{0:T(1024)} %param.13) | copy-start | bytes 98308
  7.2 71.3 %copy-start.1 = (f32[8192]{0:T(1024)S(1)}, f32[8192]{0:T(1024)}, u32[]{:S(2)}) copy-start(f32[8192]{0:T(1024)} %param.17) | copy-start | bytes 98308
  7.2 71.3 %all-reduce.3.cloned.1.call-start = ((), (), s32[]{:S(2)}) async-start(), calls=%async_computation | async-start | bytes 131072 | tf_op jit(solution)/shard_map/psum | solution.py:75
  7.2 18.4 %collective-permute-start = (bf16[1,1,8192]{2,1,0:T(2,128)(2,1)}, bf16[1,1,8192]{2,1,0:T(2,128)(2,1)S(1)}, u32[]{:S(2)}, u32[]{:S(2)}) collective-permute-start(bf16[1,1,8192]{2,1,0:T(2,128)(2,1)} %bitcast.48), channel_id=1, source_target_pairs={{0,1},{1,0},{2,3},{3,2},{4,5},{5,4},{6,7},{7,6},{8,9},{9,8},{10,11... | collective-permute-start | bytes 49160 | tf_op jit(solution)/shard_map/ppermute | solution.py:18
  29.0 4.0 %collective-permute-start.1 = (bf16[2,1,8192]{2,0,1:T(2,128)(2,1)S(1)}, bf16[2,1,8192]{2,0,1:T(2,128)(2,1)S(1)}, u32[]{:S(2)}, u32[]{:S(2)}) collective-permute-start(bf16[2,1,8192]{2,0,1:T(2,128)(2,1)S(1)} %get-tuple-element.9), channel_id=1, source_target_pairs={{0,2},{1,3},{2,0},{3,1},{4,6},{5,7},{6,4},{7,5},{8,10},{9,11},{10,... | collective-permute-start | bytes 98312 | tf_op jit(solution)/shard_map/ppermute | solution.py:18
  33.1 5.2 %collective-permute-start.2 = (bf16[4,1,8192]{2,0,1:T(4,128)(2,1)S(1)}, bf16[4,1,8192]{2,0,1:T(4,128)(2,1)S(1)}, u32[]{:S(2)}, u32[]{:S(2)}) collective-permute-start(bf16[4,1,8192]{2,0,1:T(4,128)(2,1)S(1)} %reshape.88), channel_id=1, source_target_pairs={{0,4},{1,5},{2,6},{3,7},{4,0},{5,1},{6,2},{7,3},{8,12},{9,13},{10,... | collective-permute-start | bytes 196616 | tf_op jit(solution)/shard_map/ppermute | solution.py:18
Sparse Core Ops, SparseCore 0:
  46.8 31.6 all-reduce.2
